TPU v7x, 256 devices: a whole 4x4x8 slice. The times are simulated.
256 devices in a mesh: wave: 128 (over x, y, z), par: 2 (over core).
Axes of the slice: x: 4, y: 4, z: 8, core: 2. Of those that a mesh axis runs over, the one named last changes fastest.
Arguments:
- fourier: float32 [2, 1024, 128, 256], P('par', 'wave'), may hold values from -6 to 6
- legendre: float32 [128, 2, 2000, 1024], P('wave', 'par'), may hold values from -0.1875 to 0.1875
- window_waves: int32 [128], P('wave'), may hold values from 0 to 3999, as said below
- lat_order: int32 [1024], replicated, may hold values from 0 to 1023, each once
- gauss_weights: float32 [1024], replicated, may hold values from 0.2 to 1
- mode_rates: float32 [128], replicated, may hold values from 0.5 to 20
- mode_in: float32 [128, 128], replicated, may hold values from -0.5 to 0.5
- mode_out: float32 [128, 128], replicated, may hold values from -0.5 to 0.5
Outputs:
- updated: float32 [2, 1024, 128, 256], P('par', 'wave')
Inputs may be any that keep to these rules, and one draw needn't show every extreme that they name: `window_waves`: distinct wavenumbers; 0 is always among them.
All inputs are finite; a program needn't handle non-finite values.
Results may differ from a plain program's by a relative error of at most 0.0003.
Values sent between devices are 32-bit elements; how exact they have to be, the bound alone decides.
A program may use at most 64 MiB of HBM per device.

v0:
```python
import jax
import jax.numpy as jnp
from jax import lax
from jax.sharding import PartitionSpec as P

TRUNC = 3999


precise = lax.Precision.HIGHEST


def from_partner(array, axis, distance):
    return lax.ppermute(array, axis, [(i, i ^ 1 << distance) for i in range(lax.axis_size(axis))])


def vertical(spectrum, degree, mode_rates, mode_in, mode_out):
    total_rows = spectrum.shape[0]
    levels = mode_in.shape[0]
    flattened = spectrum.reshape(total_rows * 2, levels)
    mode_vals = jnp.dot(flattened, mode_in, precision=precise, preferred_element_type=jnp.float32)
    mode_vals = mode_vals.reshape(total_rows, 2, levels)
    degree_scale = degree * (degree + 1.0) / (TRUNC * (TRUNC + 1.0))
    mode_vals = mode_vals / (1.0 + degree_scale[:, None, None] * mode_rates[None, None, :])
    returned = jnp.dot(
        mode_vals.reshape(total_rows * 2, levels),
        mode_out,
        precision=precise,
        preferred_element_type=jnp.float32,
    )
    return returned.reshape(total_rows, 2 * levels)


def transform_rows(table_rows, weighted, degree, mode_rates, mode_in, mode_out):
    live_rows = (degree <= TRUNC).astype(jnp.float32)
    spectrum = (
        jnp.dot(table_rows, weighted, precision=precise, preferred_element_type=jnp.float32)
        * live_rows[:, None]
    )
    solved = vertical(spectrum, degree.astype(jnp.float32), mode_rates, mode_in, mode_out)
    return lax.dot_general(
        table_rows,
        solved,
        (((0,), (0,)), ((), ())),
        precision=precise,
        preferred_element_type=jnp.float32,
    )


def per_device(
    fourier, legendre, window_waves, lat_order, gauss_weights, mode_rates, mode_in, mode_out
):
    parity = lax.axis_index("par")
    partner_part = from_partner(fourier, "par", 0)
    paired = jnp.where(parity == 0, fourier + partner_part, partner_part - fourier)
    owner_field = lax.all_to_all(paired, "wave", split_axis=2, concat_axis=1, tiled=True)
    field_rows = owner_field[0, :, 0, :]
    in_lat = jnp.zeros_like(field_rows).at[lat_order].set(field_rows)
    weighted = gauss_weights[:, None] * in_lat
    table = legendre[0, 0]
    wavenum = window_waves[0]
    total_rows = table.shape[0]
    degree = wavenum + parity + 2 * jnp.arange(total_rows, dtype=jnp.int32)
    grid_lat = transform_rows(table, weighted, degree, mode_rates, mode_in, mode_out)
    returned = jnp.take(grid_lat, lat_order, axis=0)[None, :, None, :]
    block_rows = lax.all_to_all(returned, "wave", split_axis=1, concat_axis=2, tiled=True)
    partner_rows = from_partner(block_rows, "par", 0)
    updated = jnp.where(parity == 0, block_rows + partner_rows, partner_rows - block_rows)
    return updated


def solution(mesh):
    return jax.shard_map(
        per_device,
        mesh=mesh,
        in_specs=(
            P("par", "wave", None, None),
            P("wave", "par", None, None),
            P("wave"),
            P(),
            P(),
            P(),
            P(),
            P(),
        ),
        out_specs=P("par", "wave", None, None),
        check_vma=False,
    )
```

profile of v0, /device:TPU:1, one launch (start us, length us, event | category | flops | bytes accessed | tf_op | source)
XLA Modules:
  0.0 137.4 jit_solution(17347047897581421894)
XLA Ops:
  0.0 0.0 copy-start
  0.0 0.0 copy-start.1
  0.0 1.9 %copy.20 = f32[1,8,128,256]{3,1,0,2:T(8,128)S(1)} copy(f32[1,8,128,256]{3,2,1,0:T(8,128)} %param.8) | data formatting | bytes 2097152 | tf_op args[0]
  1.9 3.3 %collective-permute-start = (f32[1,8,128,256]{3,1,0,2:T(8,128)S(1)}, f32[1,8,128,256]{3,1,0,2:T(8,128)S(1)}, u32[]{:S(2)}, u32[]{:S(2)}) collective-permute-start(f32[1,8,128,256]{3,1,0,2:T(8,128)S(1)} %copy.20), channel_id=1, source_target_pairs={{0,1},{1,0},{2,3},{3,2},{4,5},{5,4},{6,7},{7,6},{8,9},{9,8},{10,11... | collective-permute-start | bytes 3145736 | tf_op jit(solution)/shard_map/ppermute | solution.py:13
  5.3 0.0 copy-start.3
  5.3 0.0 copy-start.5
  5.3 2.3 %collective-permute-done = f32[1,8,128,256]{3,1,0,2:T(8,128)S(1)} collective-permute-done((f32[1,8,128,256]{3,1,0,2:T(8,128)S(1)}, f32[1,8,128,256]{3,1,0,2:T(8,128)S(1)}, u32[]{:S(2)}, u32[]{:S(2)}) %collective-permute-start) | collective-permute-done | bytes 1048608 | tf_op jit(solution)/shard_map/ppermute | solution.py:13
  7.6 0.0 copy-done.1
  7.6 1.6 %subtract_select_fusion.1 = f32[1,8,128,256]{3,1,0,2:T(8,128)} fusion(f32[1,8,128,256]{3,1,0,2:T(8,128)S(1)} %collective-permute-done, pred[]{:T(512)S(6)} %eq.4, f32[1,8,128,256]{3,2,1,0:T(8,128)S(1)} %copy-done.1), kind=kLoop, calls=%fused_computation.18 | loop fusion | flops 786432 | bytes 3145729 | tf_op jit(solution)/shard_map/jit(_where)/select_n | solution.py:54
  9.2 13.8 %all-to-all-start = ((f32[1,8,128,256]{3,1,0,2:T(8,128)}), f32[1,8,128,256]{3,1,0,2:T(8,128)S(1)}, u32[]{:S(2)}, u32[]{:S(2)}) async-start(f32[1,8,128,256]{3,1,0,2:T(8,128)} %subtract_select_fusion.1), calls=%async_computation | async-start | bytes 2097152 | tf_op jit(solution)/shard_map/all_to_all | solution.py:55
  22.9 0.0 copy-start.4
  23.7 0.0 copy-done.3
  23.7 0.0 copy-done.5
  23.7 0.3 multiply_add_fusion
  24.0 29.6 %all-to-all-done = f32[1,8,128,256]{3,1,0,2:T(8,128)S(1)} async-done(((f32[1,8,128,256]{3,1,0,2:T(8,128)}), f32[1,8,128,256]{3,1,0,2:T(8,128)S(1)}, u32[]{:S(2)}, u32[]{:S(2)}) %all-to-all-start) | async-done | bytes 1048608 | tf_op jit(solution)/shard_map/all_to_all | solution.py:55
  53.6 5.3 %scatter_custom_fusion = f32[1024,256]{1,0:T(8,128)S(1)} fusion(s32[1024]{0:T(1024)S(1)} %get-tuple-element.6, f32[1,8,128,256]{3,1,0,2:T(8,128)S(1)} %all-to-all-done, f32[]{:T(128)} %constant.14.clone.1), kind=kCustom, calls=%fused_computation.13 | custom fusion | bytes 2097156 | tf_op jit(solution)/shard_map/scatter | solution.py:57
  59.0 0.0 copy-done.4
  59.0 9.4 %fusion.9 = f32[250,2,8,128]{3,2,1,0:T(8,128)S(1)} fusion(f32[1,1,2000,1024]{3,2,1,0:T(8,128)} %param.9, f32[1024,256]{1,0:T(8,128)S(1)} %scatter_custom_fusion, f32[2000]{0:T(1024)S(1)} %fusion.23, f32[1024]{0:T(1024)S(1)} %copy-done.4), kind=kOutput, calls=%fused_computation.10 | convolution fusion | flops 6292230144 | bytes 11300672 | tf_op jit(solution)/shard_map/dot_general | solution.py:36
  68.3 0.0 copy-done
  68.3 1.9 %convolution_divide_fusion = f32[2000,2,128]{2,0,1:T(8,128)S(1)} fusion(f32[250,2,8,128]{3,2,1,0:T(8,128)S(1)} %fusion.9, f32[2000,128]{1,0:T(8,128)S(1)} %multiply_add_fusion, f32[128,128]{1,0:T(8,128)S(1)} %copy-done), kind=kOutput, calls=%fused_computation.7 | convolution fusion | flops 786944000 | bytes 5185536 | tf_op jit(solution)/shard_map/dot_general | solution.py:20
  70.2 0.0 copy-start.2
  70.2 6.4 %copy.23 = f32[2000,2,128]{2,1,0:T(2,128)S(1)} copy(f32[2000,2,128]{2,0,1:T(8,128)S(1)} %convolution_divide_fusion) | data formatting | bytes 4096000 | tf_op jit(solution)/shard_map/div | solution.py:23
  76.6 0.0 copy-done.2
  76.6 1.7 %fusion.24 = f32[4000,128]{1,0:T(8,128)S(1)} fusion(f32[4000,128]{1,0:T(8,128)S(1)} %bitcast.46, f32[128,128]{1,0:T(8,128)S(1)} %copy-done.2), kind=kOutput, calls=%fused_computation.31 | convolution fusion | flops 786432000 | bytes 4161536 | tf_op jit(solution)/shard_map/dot_general | solution.py:24
  78.4 1.9 %reshape.89 = f32[2000,256]{1,0:T(8,128)} reshape(f32[4000,128]{1,0:T(8,128)S(1)} %fusion.24) | data formatting | bytes 4096000 | tf_op jit(solution)/shard_map/reshape | solution.py:30
  80.3 9.7 %fusion.12 = f32[1024,256]{0,1:T(8,128)S(1)} fusion(f32[2000,256]{1,0:T(8,128)} %reshape.89, f32[1,1,2000,1024]{3,2,1,0:T(8,128)} %param.9), kind=kOutput, calls=%fused_computation.11 | convolution fusion | flops 6291456000 | bytes 11288576 | tf_op jit(solution)/shard_map/dot_general | solution.py:40
  90.0 0.3 copy.24
  90.4 3.5 %gather_fusion = f32[1024,256]{1,0:T(8,128)S(1)} fusion(f32[1024,256]{1,0:T(8,128)S(1)} %copy.24, s32[1024]{0:T(1024)S(1)} %get-tuple-element.5), kind=kCustom, calls=%fused_computation | custom fusion | bytes 2101248 | tf_op jit(solution)/shard_map/jit(_take)/gather | solution.py:64
  93.8 0.2 bitcast_select_fusion
  94.0 1.1 copy.25
  95.1 34.6 %all_to_all.33 = f32[1,1024,1,256]{3,2,0,1:T(1,128)S(1)} all-to-all(f32[1,1024,1,256]{3,2,0,1:T(1,128)S(1)} %copy.25), channel_id=1, replica_groups=mesh['wave'=128,'par'=2] {'wave'}, dimensions={1} | all-to-all | bytes 2097152 | tf_op jit(solution)/shard_map/all_to_all | solution.py:65
  129.7 0.1 copy.37
  129.8 3.9 %collective-permute-start.1 = (f32[1,8,128,256]{3,1,0,2:T(8,128)S(1)}, f32[1,8,128,256]{3,1,0,2:T(8,128)S(1)}, u32[]{:S(2)}, u32[]{:S(2)}) collective-permute-start(f32[1,8,128,256]{3,1,0,2:T(8,128)S(1)} %bitcast.47), channel_id=1, source_target_pairs={{0,1},{1,0},{2,3},{3,2},{4,5},{5,4},{6,7},{7,6},{8,9},{9,8},{10,11... | collective-permute-start | bytes 3145736 | tf_op jit(solution)/shard_map/ppermute | solution.py:13
  133.7 2.3 %collective-permute-done.1 = f32[1,8,128,256]{3,1,0,2:T(8,128)S(1)} collective-permute-done((f32[1,8,128,256]{3,1,0,2:T(8,128)S(1)}, f32[1,8,128,256]{3,1,0,2:T(8,128)S(1)}, u32[]{:S(2)}, u32[]{:S(2)}) %collective-permute-start.1) | collective-permute-done | bytes 1048608 | tf_op jit(solution)/shard_map/ppermute | solution.py:13
  136.0 0.1 subtract_select_fusion
  136.1 1.3 copy.26
  (4 shorter events, 0.0 us)
Async XLA Ops:
  0.0 68.3 %copy-start = (f32[128,128]{1,0:T(8,128)S(1)}, f32[128,128]{1,0:T(8,128)}, u32[]{:S(2)}) copy-start(f32[128,128]{1,0:T(8,128)} %param.14) | copy-start | bytes 196612
  0.0 7.5 %copy-start.1 = (f32[1,8,128,256]{3,2,1,0:T(8,128)S(1)}, f32[1,8,128,256]{3,2,1,0:T(8,128)}, u32[]{:S(2)}) copy-start(f32[1,8,128,256]{3,2,1,0:T(8,128)} %param.8) | copy-start | bytes 3145732
  1.9 5.6 %collective-permute-start = (f32[1,8,128,256]{3,1,0,2:T(8,128)S(1)}, f32[1,8,128,256]{3,1,0,2:T(8,128)S(1)}, u32[]{:S(2)}, u32[]{:S(2)}) collective-permute-start(f32[1,8,128,256]{3,1,0,2:T(8,128)S(1)} %copy.20), channel_id=1, source_target_pairs={{0,1},{1,0},{2,3},{3,2},{4,5},{5,4},{6,7},{7,6},{8,9},{9,8},{10,11... | collective-permute-start | bytes 3145736 | tf_op jit(solution)/shard_map/ppermute | solution.py:13
  5.3 18.4 %copy-start.3 = (s32[1024]{0:T(1024)S(1)}, s32[1024]{0:T(1024)}, u32[]{:S(2)}) copy-start(s32[1024]{0:T(1024)} %param.11) | copy-start | bytes 12292
  5.3 18.4 %copy-start.5 = (f32[128]{0:T(128)S(1)}, f32[128]{0:T(128)}, u32[]{:S(2)}) copy-start(f32[128]{0:T(128)} %param.13) | copy-start | bytes 1540
  9.2 44.5 %all-to-all-start = ((f32[1,8,128,256]{3,1,0,2:T(8,128)}), f32[1,8,128,256]{3,1,0,2:T(8,128)S(1)}, u32[]{:S(2)}, u32[]{:S(2)}) async-start(f32[1,8,128,256]{3,1,0,2:T(8,128)} %subtract_select_fusion.1), calls=%async_computation | async-start | bytes 2097152 | tf_op jit(solution)/shard_map/all_to_all | solution.py:55
  22.9 36.0 %copy-start.4 = (f32[1024]{0:T(1024)S(1)}, f32[1024]{0:T(1024)}, u32[]{:S(2)}) copy-start(f32[1024]{0:T(1024)} %param.12) | copy-start | bytes 12292
  70.2 6.4 %copy-start.2 = (f32[128,128]{1,0:T(8,128)S(1)}, f32[128,128]{1,0:T(8,128)}, u32[]{:S(2)}) copy-start(f32[128,128]{1,0:T(8,128)} %param.15) | copy-start | bytes 196612
  129.8 6.2 %collective-permute-start.1 = (f32[1,8,128,256]{3,1,0,2:T(8,128)S(1)}, f32[1,8,128,256]{3,1,0,2:T(8,128)S(1)}, u32[]{:S(2)}, u32[]{:S(2)}) collective-permute-start(f32[1,8,128,256]{3,1,0,2:T(8,128)S(1)} %bitcast.47), channel_id=1, source_target_pairs={{0,1},{1,0},{2,3},{3,2},{4,5},{5,4},{6,7},{7,6},{8,9},{9,8},{10,11... | collective-permute-start | bytes 3145736 | tf_op jit(solution)/shard_map/ppermute | solution.py:13
where the time goes:
time: 138 us; the launch traced here: 137 us
  blocking collectives  34.6 us (25%)
  waiting for transfers between devices  34.2 us (25%)
  matrix products  22.7 us (16%)
  local copies, waits for them, and re-layouts  21.8 us (16%)
  starting transfers between devices  21 us (15%)
  other arithmetic  2.31 us (2%)
    all_to_all x1, blocking collectives, per_device(): lax.all_to_all(returned, 'wave', split_axis=1, concat_axis=2, tiled=True)  34.6 us
    all_to_all x1, waiting for transfers between devices, per_device(): lax.all_to_all(paired, 'wave', split_axis=2, concat_axis=1, tiled=True)  29.6 us
    all_to_all x1, starting transfers between devices, per_device(): lax.all_to_all(paired, 'wave', split_axis=2, concat_axis=1, tiled=True)  13.8 us
    dot_general x1, matrix products, transform_rows(): lax.dot_general(table_rows, solved, (((0,), (0,)), ((), ())), precision=p...  9.72 us
    dot_general x1, matrix products, transform_rows(): jnp.dot(table_rows, weighted, precision=precise, preferred_element_type=j...  9.35 us
    ppermute x2, starting transfers between devices, from_partner(): lax.ppermute(array, axis, [(i, i ^ 1 << distance) for i in range(lax.axis...  7.24 us
    div x1, local copies, waits for them, and re-layouts, vertical(): mode_vals / (1.0 + degree_scale[:, None, None] * mode_rates[None, None, :])  6.37 us
    scatter x1, local copies, waits for them, and re-layouts, per_device(): in_lat = jnp.zeros_like(field_rows).at[lat_order].set(field_rows)  5.29 us
  transfers between devices with their start and end apart: 3, of which 3 were waited for; matrix products, arithmetic and copies ran while one was open for 0% of the time, Pallas kernels for 0%

commit v1 on v0

v1 whole, which is shorter than its diff:
```python
import functools

import jax
import jax.numpy as jnp
from jax import lax
from jax.experimental import pallas as pl
from jax.experimental.pallas import tpu as pltpu
from jax.sharding import PartitionSpec as P

TRUNC = 3999
LANES = 128
precise = lax.Precision.HIGHEST
MESH = pl.DeviceIdType.MESH
f32, bf16 = jnp.float32, jnp.bfloat16


def at_offset(me, k, n):
    if n != 128:
        return (me + k) % n
    x, y, z = me // 32, (me // 8) % 4, me % 8
    dx, dy, dz = k // 32, (k // 8) % 4, k % 8
    return ((x + dx) % 4) * 32 + ((y + dy) % 4) * 8 + (z + dz) % 8


def split(value):
    high = value.astype(bf16)
    return high, (value - high.astype(f32)).astype(bf16)


def mm(a, b):
    return jnp.dot(a, b, preferred_element_type=f32)


def mm_nt(a, b, precision=None):
    return lax.dot_general(
        a, b, (((1,), (1,)), ((), ())), precision=precision, preferred_element_type=f32
    )


def step_kernel(
    n, wave_ref, field_hbm, table_hbm, order_ref, gauss_ref, rates_ref, in_ref, out_mat_ref,
    result,
    field, table, high, low, pick, place, gauss_col, out_t,
    send, recv, other, stack, weighted, solved_t, grid_t, back, back_other, send_out,
    field_sem, table_sem, in_send, in_recv, pair_send, pair_recv,
    out_send, out_recv, back_send, back_recv, own_sem,
):
    me = lax.axis_index("wave")
    par = lax.axis_index("par")
    lats = 8 * n
    slots = table.shape[0]
    padded = high.shape[0]
    tile = min(256, lats)
    jtile = 256
    sign = (1 - 2 * par).astype(f32)
    partner = {"par": 1 - par}

    barrier = pltpu.get_barrier_semaphore()
    field_in = [
        pltpu.make_async_copy(
            field_hbm.at[:, pl.ds(h * LANES, LANES)], field.at[h], field_sem.at[h]
        )
        for h in range(2)
    ]
    for copy in field_in:
        copy.start()
    table_in = pltpu.make_async_copy(table_hbm, table, table_sem)
    table_in.start()
    pl.semaphore_signal(barrier, inc=1, device_id=partner, device_id_type=MESH)

    @pl.loop(1, n)
    def _(k):
        pl.semaphore_signal(
            barrier, inc=1, device_id={"wave": at_offset(me, k, n)}, device_id_type=MESH
        )

    for h in range(2):
        field_in[h].wait()

        @pl.loop(0, n)
        def _(w, h=h):
            send[h, w] = field[h, pl.ds(w, 8, stride=n), :]

        recv[h, pl.ds(me, 1)] = send[h, pl.ds(me, 1)]

    pl.semaphore_wait(barrier, n)

    def send_all(source, target, send_sem, recv_sem, h):
        @pl.loop(1, n)
        def _(k):
            d = at_offset(me, k, n)
            pltpu.make_async_remote_copy(
                src_ref=source.at[h, d],
                dst_ref=target.at[h, me],
                send_sem=send_sem.at[h],
                recv_sem=recv_sem.at[h],
                device_id={"wave": d},
                device_id_type=MESH,
            ).start()

    def all_of(source, target, send_sem, recv_sem, h):
        return pltpu.make_async_remote_copy(
            src_ref=source.at[h, pl.ds(0, n - 1)],
            dst_ref=target.at[h, pl.ds(0, n - 1)],
            send_sem=send_sem.at[h],
            recv_sem=recv_sem.at[h],
            device_id=partner,
            device_id_type=MESH,
        )

    for h in range(2):
        send_all(send, recv, in_send, in_recv, h)

    for t in range(lats // LANES):
        rows = pl.ds(t * LANES, LANES)
        gauss_col[rows, :] = jnp.broadcast_to(gauss_ref[t : t + 1, :], (LANES, LANES)).T
        order_t = jnp.broadcast_to(order_ref[t : t + 1, :].astype(f32), (LANES, LANES)).T
        order_t = order_t.astype(jnp.int32)
        for c in range(lats // LANES):
            lat = lax.broadcasted_iota(jnp.int32, (LANES, LANES), 1) + c * LANES
            pick[rows, pl.ds(c * LANES, LANES)] = jnp.where(order_t == lat, 1.0, 0.0).astype(bf16)

    @pl.loop(0, lats // LANES)
    def _(c):
        lat = lax.broadcasted_iota(jnp.int32, (LANES, LANES), 0) + c * LANES
        for t in range(lats // LANES):
            same = order_ref[t : t + 1, :] == lat
            place[pl.ds(pl.multiple_of(c * LANES, LANES), LANES), pl.ds(t * LANES, LANES)] = (
                jnp.where(same, 1.0, 0.0).astype(bf16)
            )

    out_t[...] = out_mat_ref[...].T
    table_in.wait()

    @pl.loop(0, slots // 16)
    def _(c):
        rows = pl.ds(pl.multiple_of(c * 16, 16), 16)
        high[rows, :], low[rows, :] = split(table[rows, :])

    rest = padded - slots
    high[pl.ds(slots, rest), :] = jnp.zeros((rest, lats), bf16)
    low[pl.ds(slots, rest), :] = jnp.zeros((rest, lats), bf16)

    @pl.loop(0, 2)
    def _(h):
        all_of(send, recv, in_send, in_recv, h).wait_recv()
        pair = pltpu.make_async_remote_copy(
            src_ref=recv.at[h], dst_ref=other.at[h], send_sem=pair_send.at[h],
            recv_sem=pair_recv.at[h], device_id=partner, device_id_type=MESH,
        )
        pair.start()
        pair.wait()

        @pl.loop(0, lats // tile)
        def _(t):
            blocks = pl.ds(t * (tile // 8), tile // 8)
            paired = other[h, blocks] + sign * recv[h, blocks]
            rows = pl.ds(pl.multiple_of(t * tile, tile), tile)
            stack[rows, :LANES], stack[rows, LANES:] = split(paired.reshape(tile, LANES))

        @pl.loop(0, lats // tile)
        def _(t):
            rows = pl.ds(pl.multiple_of(t * tile, tile), tile)
            both = mm(place[rows, :], stack[...])
            scaled = (both[:, :LANES] + both[:, LANES:]) * gauss_col[rows, :]
            weighted[rows, :LANES], weighted[rows, LANES:] = split(scaled)

        @pl.loop(0, padded // jtile)
        def _(t):
            rows = pl.ds(pl.multiple_of(t * jtile, jtile), jtile)
            both = mm(high[rows, :], weighted[...])
            summed = both[:, :LANES] + both[:, LANES:] + mm(low[rows, :], weighted[:, :LANES])
            slot = lax.broadcasted_iota(jnp.int32, (jtile, LANES), 0) + t * jtile
            degree = wave_ref[0] + par + 2 * slot
            spectrum = jnp.where(degree <= TRUNC, summed, 0.0)
            modes = jnp.dot(spectrum, in_ref[...], precision=precise, preferred_element_type=f32)
            degree = degree.astype(f32)
            scale = degree * (degree + 1.0) / (TRUNC * (TRUNC + 1.0))
            modes = modes / (1.0 + scale * rates_ref[...])
            solved = mm_nt(out_t[...], modes, precise)
            solved_t[:LANES, rows], solved_t[LANES:, rows] = split(solved)

        @pl.loop(0, lats // tile)
        def _(t):
            cols = pl.ds(pl.multiple_of(t * tile, tile), tile)
            both = mm(solved_t[...], high[:, cols])
            grid = both[:LANES] + both[LANES:] + mm(solved_t[:LANES, :], low[:, cols])
            grid_t[:LANES, cols], grid_t[LANES:, cols] = split(grid)

        @pl.loop(0, lats // tile)
        def _(t):
            rows = pl.ds(pl.multiple_of(t * tile, tile), tile)
            both = mm_nt(pick[rows, :], grid_t[...])
            back[h, pl.ds(t * (tile // 8), tile // 8)] = (
                both[:, :LANES] + both[:, LANES:]
            ).reshape(tile // 8, 8, LANES)

        swap = pltpu.make_async_remote_copy(
            src_ref=back.at[h], dst_ref=back_other.at[h], send_sem=back_send.at[h],
            recv_sem=back_recv.at[h], device_id=partner, device_id_type=MESH,
        )
        swap.start()
        swap.wait()

        @pl.loop(0, n // 8)
        def _(t):
            blocks = pl.ds(t * 8, 8)
            send_out[h, blocks] = back_other[h, blocks] + sign * back[h, blocks]

        send_all(send_out, result, out_send, out_recv, h)
        pltpu.make_async_copy(send_out.at[h, me], result.at[h, me], own_sem.at[h]).start()

    for h in range(2):
        pltpu.make_async_copy(send_out.at[h, me], result.at[h, me], own_sem.at[h]).wait()
        all_of(send, recv, in_send, in_recv, h).wait_send()
        all_of(send_out, result, out_send, out_recv, h).wait()


def per_device(
    fourier, legendre, window_waves, lat_order, gauss_weights, mode_rates, mode_in, mode_out
):
    n = lax.axis_size("wave")
    lats = gauss_weights.shape[0]
    slots = legendre.shape[2]
    padded = -(-slots // 256) * 256
    vmem = pl.BlockSpec(memory_space=pltpu.VMEM)
    anywhere = pl.BlockSpec(memory_space=pl.ANY)
    blocks = pltpu.VMEM((2, n, 8, LANES), f32)
    dma2 = pltpu.SemaphoreType.DMA((2,))
    flops = 24 * slots * lats * LANES
    out = pl.pallas_call(
        functools.partial(step_kernel, n),
        out_shape=jax.ShapeDtypeStruct((2, n, 8, LANES), f32),
        in_specs=[pl.BlockSpec(memory_space=pltpu.SMEM), anywhere, anywhere] + [vmem] * 5,
        out_specs=anywhere,
        scratch_shapes=[
            pltpu.VMEM((2, lats, LANES), f32),
            pltpu.VMEM((slots, lats), f32),
            pltpu.VMEM((padded, lats), bf16),
            pltpu.VMEM((padded, lats), bf16),
            pltpu.VMEM((lats, lats), bf16),
            pltpu.VMEM((lats, lats), bf16),
            pltpu.VMEM((lats, LANES), f32),
            pltpu.VMEM((LANES, LANES), f32),
            blocks,
            blocks,
            blocks,
            pltpu.VMEM((lats, 2 * LANES), bf16),
            pltpu.VMEM((lats, 2 * LANES), bf16),
            pltpu.VMEM((2 * LANES, padded), bf16),
            pltpu.VMEM((2 * LANES, lats), bf16),
            blocks,
            blocks,
            blocks,
            dma2,
            pltpu.SemaphoreType.DMA,
        ]
        + [dma2] * 9,
        compiler_params=pltpu.CompilerParams(
            collective_id=0, has_side_effects=True, vmem_limit_bytes=56 << 20
        ),
        cost_estimate=pl.CostEstimate(
            flops=flops, bytes_accessed=slots * lats * 4, transcendentals=0
        ),
        name="spectral_step",
    )(
        window_waves,
        fourier.reshape(8 * n, 2 * LANES),
        legendre[0, 0],
        lat_order.reshape(lats // LANES, LANES),
        gauss_weights.reshape(lats // LANES, LANES),
        mode_rates.reshape(1, LANES),
        mode_in,
        mode_out,
    )
    return out.transpose(2, 1, 0, 3).reshape(1, 8, n, 2 * LANES)


def solution(mesh):
    return jax.shard_map(
        per_device,
        mesh=mesh,
        in_specs=(
            P("par", "wave", None, None),
            P("wave", "par", None, None),
            P("wave"),
            P(),
            P(),
            P(),
            P(),
            P(),
        ),
        out_specs=P("par", "wave", None, None),
        check_vma=False,
    )
```

time: 138 us -> 92.2 us (0.67)
  Pallas kernels: 0 us -> 88.5 us
  blocking collectives: 34.6 us -> 0 us
  waiting for transfers between devices: 34.2 us -> 0 us
  matrix products: 22.7 us -> 0 us
  starting transfers between devices: 21 us -> 0 us
  local copies, waits for them, and re-layouts: 21.8 us -> 2.87 us
  other arithmetic: 2.31 us -> 0 us
    pallas_call x0 -> x1, Pallas kernels: none -> 88.5 us  [per_device(): pl.pallas_call(functools.partial(step_kernel, n), out_shape=jax.ShapeDtyp...]
    all_to_all x1 -> x0, blocking collectives: 34.6 us -> none  [per_device(): lax.all_to_all(returned, 'wave', split_axis=1, concat_axis=2, tiled=True)]
    all_to_all x1 -> x0, waiting for transfers between devices: 29.6 us -> none  [per_device(): lax.all_to_all(paired, 'wave', split_axis=2, concat_axis=1, tiled=True)]
    dot_general x4 -> x0, matrix products: 22.7 us -> none  [the longest x1 9.72 us: transform_rows(): lax.dot_general(table_rows, solved, (((0,), (0,)), ((), ())), precision=p...]
    all_to_all x1 -> x0, starting transfers between devices: 13.8 us -> none  [per_device(): lax.all_to_all(paired, 'wave', split_axis=2, concat_axis=1, tiled=True)]
    ppermute x2 -> x0, starting transfers between devices: 7.24 us -> none  [from_partner(): lax.ppermute(array, axis, [(i, i ^ 1 << distance) for i in range(lax.axis...]
    div x1 -> x0, local copies, waits for them, and re-layouts: 6.37 us -> none  [vertical(): mode_vals / (1.0 + degree_scale[:, None, None] * mode_rates[None, None, :])]
    scatter x1 -> x0, local copies, waits for them, and re-layouts: 5.29 us -> none  [per_device(): in_lat = jnp.zeros_like(field_rows).at[lat_order].set(field_rows)]
  transfers between devices with their start and end apart: 3 -> 0, of which waited for: 3 -> 0; matrix products, arithmetic and copies ran while one was open for 0% -> 0% of each run, Pallas kernels for 0% -> 0%
where the time goes in v1:
time: 92.2 us; the launch traced here: 92 us
  Pallas kernels  88.5 us (96%)
  local copies, waits for them, and re-layouts  2.87 us (3%)
    pallas_call x1, Pallas kernels, per_device(): pl.pallas_call(functools.partial(step_kernel, n), out_shape=jax.ShapeDtyp...  88.5 us

profile of v1, /device:TPU:1, one launch (start us, length us, event | category | flops | bytes accessed | tf_op | source)
XLA Modules:
  0.0 92.0 jit_solution(9034206080328240566)
XLA Ops:
  0.7 88.5 %spectral_step.1 = f32[2,128,8,128]{3,2,1,0:T(8,128)} custom-call(s32[1]{0:T(128)S(6)} %copy.11.wave_ref, f32[1024,256]{1,0:T(8,128)} %bitcast.10, f32[2000,1024]{1,0:T(8,128)} %bitcast.9, s32[8,128]{1,0:T(8,128)} %bitcast.11, f32[8,128]{1,0:T(8,128)} %bitcast.12, f32[1,128]{1,0:T(1,128)} %bitcast.13, f32[128,128]{1,0:T(8,128)} %in_ref.1, f32[128,128]{1,0:T(8,128)} %out_mat_ref.1), custom_call_target="tpu_custom_call" | custom-call | flops 6291456000 | bytes 8192000 | tf_op jit(solution)/shard_map/spectral_step/pallas_call | solution.py:231
  89.1 1.6 %copy.9 = f32[8,128,2,128]{1,3,2,0:T(8,128)S(1)} copy(f32[8,128,2,128]{3,0,1,2:T(8,128)} %bitcast.8) | data formatting | bytes 2097152 | tf_op jit(solution)/shard_map/transpose | solution.py:276
  90.7 1.3 %copy.10 = f32[1,8,128,256]{3,2,1,0:T(8,128)} copy(f32[1,8,128,256]{2,3,1,0:T(8,128)S(1)} %bitcast.7) | data formatting | bytes 2097152 | tf_op jit(solution)/shard_map/reshape | solution.py:276

commit v2 on v1

--- a/solution.py
+++ b/solution.py
@@ -9,7 +9,6 @@
 
 TRUNC = 3999
 LANES = 128
-precise = lax.Precision.HIGHEST
 MESH = pl.DeviceIdType.MESH
 f32, bf16 = jnp.float32, jnp.bfloat16
 
@@ -31,17 +30,15 @@
     return jnp.dot(a, b, preferred_element_type=f32)
 
 
-def mm_nt(a, b, precision=None):
-    return lax.dot_general(
-        a, b, (((1,), (1,)), ((), ())), precision=precision, preferred_element_type=f32
-    )
+def mm_nt(a, b):
+    return lax.dot_general(a, b, (((1,), (1,)), ((), ())), preferred_element_type=f32)
 
 
 def step_kernel(
     n, wave_ref, field_hbm, table_hbm, order_ref, gauss_ref, rates_ref, in_ref, out_mat_ref,
     result,
-    field, table, high, low, pick, place, gauss_col, out_t,
-    send, recv, other, stack, weighted, solved_t, grid_t, back, back_other, send_out,
+    field, table, high, low, pick, place, gauss_col, in_terms, out_terms,
+    send, recv, other, stack, weighted, terms, solved_t, grid_t, back, back_other, send_out,
     field_sem, table_sem, in_send, in_recv, pair_send, pair_recv,
     out_send, out_recv, back_send, back_recv, own_sem,
 ):
@@ -51,7 +48,7 @@
     slots = table.shape[0]
     padded = high.shape[0]
     tile = min(256, lats)
-    jtile = 256
+    jtile, vtile, ctile, ltile = min(1024, padded), min(1024, padded), min(512, lats), min(1024, lats)
     sign = (1 - 2 * par).astype(f32)
     partner = {"par": 1 - par}
 
@@ -129,7 +126,12 @@
                 jnp.where(same, 1.0, 0.0).astype(bf16)
             )
 
-    out_t[...] = out_mat_ref[...].T
+    in_high, in_low = split(in_ref[...])
+    in_terms[:LANES, :LANES], in_terms[:LANES, LANES:] = in_high, in_low
+    in_terms[LANES:, :LANES], in_terms[LANES:, LANES:] = in_high, jnp.zeros_like(in_low)
+    out_high, out_low = split(out_mat_ref[...].T)
+    out_terms[:LANES, :LANES], out_terms[:LANES, LANES:] = out_high, out_high
+    out_terms[LANES:, :LANES], out_terms[LANES:, LANES:] = out_low, jnp.zeros_like(out_low)
     table_in.wait()
 
     @pl.loop(0, slots // 16)
@@ -141,16 +143,21 @@
     high[pl.ds(slots, rest), :] = jnp.zeros((rest, lats), bf16)
     low[pl.ds(slots, rest), :] = jnp.zeros((rest, lats), bf16)
 
-    @pl.loop(0, 2)
-    def _(h):
-        all_of(send, recv, in_send, in_recv, h).wait_recv()
-        pair = pltpu.make_async_remote_copy(
+    def pair_of(h):
+        return pltpu.make_async_remote_copy(
             src_ref=recv.at[h], dst_ref=other.at[h], send_sem=pair_send.at[h],
             recv_sem=pair_recv.at[h], device_id=partner, device_id_type=MESH,
         )
-        pair.start()
-        pair.wait()
-
+
+    def swap_of(h, t):
+        blocks = pl.ds(t * (tile // 8), tile // 8)
+        return pltpu.make_async_remote_copy(
+            src_ref=back.at[h, blocks], dst_ref=back_other.at[h, blocks],
+            send_sem=back_send.at[h, t], recv_sem=back_recv.at[h, t],
+            device_id=partner, device_id_type=MESH,
+        )
+
+    def solve(h):
         @pl.loop(0, lats // tile)
         def _(t):
             blocks = pl.ds(t * (tile // 8), tile // 8)
@@ -158,9 +165,8 @@
             rows = pl.ds(pl.multiple_of(t * tile, tile), tile)
             stack[rows, :LANES], stack[rows, LANES:] = split(paired.reshape(tile, LANES))
 
-        @pl.loop(0, lats // tile)
-        def _(t):
-            rows = pl.ds(pl.multiple_of(t * tile, tile), tile)
+        for t in range(lats // ltile):
+            rows = pl.ds(t * ltile, ltile)
             both = mm(place[rows, :], stack[...])
             scaled = (both[:, :LANES] + both[:, LANES:]) * gauss_col[rows, :]
             weighted[rows, :LANES], weighted[rows, LANES:] = split(scaled)
@@ -173,45 +179,58 @@
             slot = lax.broadcasted_iota(jnp.int32, (jtile, LANES), 0) + t * jtile
             degree = wave_ref[0] + par + 2 * slot
             spectrum = jnp.where(degree <= TRUNC, summed, 0.0)
-            modes = jnp.dot(spectrum, in_ref[...], precision=precise, preferred_element_type=f32)
-            degree = degree.astype(f32)
+            terms[rows, :LANES], terms[rows, LANES:] = split(spectrum)
+
+        @pl.loop(0, padded // vtile)
+        def _(t):
+            rows = pl.ds(pl.multiple_of(t * vtile, vtile), vtile)
+            slot = lax.broadcasted_iota(jnp.int32, (vtile, LANES), 0) + t * vtile
+            degree = (wave_ref[0] + par + 2 * slot).astype(f32)
+            both = mm(terms[rows, :], in_terms[...])
             scale = degree * (degree + 1.0) / (TRUNC * (TRUNC + 1.0))
-            modes = modes / (1.0 + scale * rates_ref[...])
-            solved = mm_nt(out_t[...], modes, precise)
-            solved_t[:LANES, rows], solved_t[LANES:, rows] = split(solved)
-
-        @pl.loop(0, lats // tile)
+            modes = (both[:, :LANES] + both[:, LANES:]) / (1.0 + scale * rates_ref[...])
+            modes = jnp.concatenate(split(modes), axis=1)
+            both = mm_nt(out_terms[...], modes)
+            solved_t[:LANES, rows], solved_t[LANES:, rows] = split(both[:LANES] + both[LANES:])
+
+        @pl.loop(0, lats // ctile)
         def _(t):
-            cols = pl.ds(pl.multiple_of(t * tile, tile), tile)
+            cols = pl.ds(pl.multiple_of(t * ctile, ctile), ctile)
             both = mm(solved_t[...], high[:, cols])
             grid = both[:LANES] + both[LANES:] + mm(solved_t[:LANES, :], low[:, cols])
             grid_t[:LANES, cols], grid_t[LANES:, cols] = split(grid)
 
-        @pl.loop(0, lats // tile)
-        def _(t):
-            rows = pl.ds(pl.multiple_of(t * tile, tile), tile)
-            both = mm_nt(pick[rows, :], grid_t[...])
+        for t in range(lats // tile):
+            both = mm_nt(pick[pl.ds(t * tile, tile), :], grid_t[...])
             back[h, pl.ds(t * (tile // 8), tile // 8)] = (
                 both[:, :LANES] + both[:, LANES:]
             ).reshape(tile // 8, 8, LANES)
-
-        swap = pltpu.make_async_remote_copy(
-            src_ref=back.at[h], dst_ref=back_other.at[h], send_sem=back_send.at[h],
-            recv_sem=back_recv.at[h], device_id=partner, device_id_type=MESH,
-        )
-        swap.start()
-        swap.wait()
-
-        @pl.loop(0, n // 8)
-        def _(t):
-            blocks = pl.ds(t * 8, 8)
+            swap_of(h, t).start()
+
+    def send_back(h):
+        for t in range(lats // tile):
+            swap_of(h, t).wait()
+            blocks = pl.ds(t * (tile // 8), tile // 8)
             send_out[h, blocks] = back_other[h, blocks] + sign * back[h, blocks]
-
         send_all(send_out, result, out_send, out_recv, h)
-        pltpu.make_async_copy(send_out.at[h, me], result.at[h, me], own_sem.at[h]).start()
+        own_out(h).start()
+
+    def own_out(h):
+        return pltpu.make_async_copy(send_out.at[h, me], result.at[h, me], own_sem.at[h])
+
+    all_of(send, recv, in_send, in_recv, 0).wait_recv()
+    pair_of(0).start()
+    pair_of(0).wait()
+    solve(0)
+    send_back(0)
+    all_of(send, recv, in_send, in_recv, 1).wait_recv()
+    pair_of(1).start()
+    pair_of(1).wait()
+    solve(1)
+    send_back(1)
 
     for h in range(2):
-        pltpu.make_async_copy(send_out.at[h, me], result.at[h, me], own_sem.at[h]).wait()
+        own_out(h).wait()
         all_of(send, recv, in_send, in_recv, h).wait_send()
         all_of(send_out, result, out_send, out_recv, h).wait()
 
@@ -241,12 +260,14 @@
             pltpu.VMEM((lats, lats), bf16),
             pltpu.VMEM((lats, lats), bf16),
             pltpu.VMEM((lats, LANES), f32),
-            pltpu.VMEM((LANES, LANES), f32),
+            pltpu.VMEM((2 * LANES, 2 * LANES), bf16),
+            pltpu.VMEM((2 * LANES, 2 * LANES), bf16),
             blocks,
             blocks,
             blocks,
             pltpu.VMEM((lats, 2 * LANES), bf16),
             pltpu.VMEM((lats, 2 * LANES), bf16),
+            pltpu.VMEM((padded, 2 * LANES), bf16),
             pltpu.VMEM((2 * LANES, padded), bf16),
             pltpu.VMEM((2 * LANES, lats), bf16),
             blocks,
@@ -255,7 +276,9 @@
             dma2,
             pltpu.SemaphoreType.DMA,
         ]
-        + [dma2] * 9,
+        + [dma2] * 6
+        + [pltpu.SemaphoreType.DMA((2, 4))] * 2
+        + [dma2],
         compiler_params=pltpu.CompilerParams(
             collective_id=0, has_side_effects=True, vmem_limit_bytes=56 << 20
         ),

time: 92.2 us -> 80.2 us (0.87)
  Pallas kernels: 88.5 us -> 76.5 us
    pallas_call x1, Pallas kernels: 88.5 us -> 76.5 us  [per_device(): pl.pallas_call(functools.partial(step_kernel, n), out_shape=jax.ShapeDtyp...]
where the time goes in v2:
time: 80.2 us; the launch traced here: 80 us
  Pallas kernels  76.5 us (95%)
  local copies, waits for them, and re-layouts  2.87 us (4%)
    pallas_call x1, Pallas kernels, per_device(): pl.pallas_call(functools.partial(step_kernel, n), out_shape=jax.ShapeDtyp...  76.5 us

profile of v2, /device:TPU:1, one launch (start us, length us, event | category | flops | bytes accessed | tf_op | source)
XLA Modules:
  0.0 80.0 jit_solution(5953456668920632949)
XLA Ops:
  0.7 76.5 %spectral_step.1 = f32[2,128,8,128]{3,2,1,0:T(8,128)} custom-call(s32[1]{0:T(128)S(6)} %copy.11.wave_ref, f32[1024,256]{1,0:T(8,128)} %bitcast.10, f32[2000,1024]{1,0:T(8,128)} %bitcast.9, s32[8,128]{1,0:T(8,128)} %bitcast.11, f32[8,128]{1,0:T(8,128)} %bitcast.12, f32[1,128]{1,0:T(1,128)} %bitcast.13, f32[128,128]{1,0:T(8,128)} %in_ref.1, f32[128,128]{1,0:T(8,128)} %out_mat_ref.1), custom_call_target="tpu_custom_call" | custom-call | flops 6291456000 | bytes 8192000 | tf_op jit(solution)/shard_map/spectral_step/pallas_call | solution.py:250
  77.2 1.6 %copy.9 = f32[8,128,2,128]{1,3,2,0:T(8,128)S(1)} copy(f32[8,128,2,128]{3,0,1,2:T(8,128)} %bitcast.8) | data formatting | bytes 2097152 | tf_op jit(solution)/shard_map/transpose | solution.py:299
  78.7 1.3 %copy.10 = f32[1,8,128,256]{3,2,1,0:T(8,128)} copy(f32[1,8,128,256]{2,3,1,0:T(8,128)S(1)} %bitcast.7) | data formatting | bytes 2097152 | tf_op jit(solution)/shard_map/reshape | solution.py:299

commit v3 on v2

--- a/solution.py
+++ b/solution.py
@@ -13,12 +13,21 @@
 f32, bf16 = jnp.float32, jnp.bfloat16
 
 
-def at_offset(me, k, n):
-    if n != 128:
-        return (me + k) % n
-    x, y, z = me // 32, (me // 8) % 4, me % 8
-    dx, dy, dz = k // 32, (k // 8) % 4, k % 8
-    return ((x + dx) % 4) * 32 + ((y + dy) % 4) * 8 + (z + dz) % 8
+def each_peer(me, n, visit):
+    group, z = lax.div(me, 8), lax.rem(me, 8)
+    near = [z] + [lax.rem(z + dz, 8) for dz in range(1, 8)]
+    for dz in range(1, 8):
+        visit(group * 8 + near[dz])
+
+    @pl.loop(1, n // 8)
+    def _(g):
+        if n == 128:
+            x, y = lax.div(group, 4), lax.rem(group, 4)
+            there = lax.rem(x + lax.div(g, 4), 4) * 4 + lax.rem(y + lax.rem(g, 4), 4)
+        else:
+            there = lax.rem(group + g, n // 8)
+        for dz in range(8):
+            visit(there * 8 + near[dz])
 
 
 def split(value):
@@ -65,16 +74,15 @@
     table_in.start()
     pl.semaphore_signal(barrier, inc=1, device_id=partner, device_id_type=MESH)
 
-    @pl.loop(1, n)
-    def _(k):
-        pl.semaphore_signal(
-            barrier, inc=1, device_id={"wave": at_offset(me, k, n)}, device_id_type=MESH
-        )
+    def greet(d):
+        pl.semaphore_signal(barrier, inc=1, device_id={"wave": d}, device_id_type=MESH)
+
+    each_peer(me, n, greet)
 
     for h in range(2):
         field_in[h].wait()
 
-        @pl.loop(0, n)
+        @pl.loop(0, n, unroll=8)
         def _(w, h=h):
             send[h, w] = field[h, pl.ds(w, 8, stride=n), :]
 
@@ -83,9 +91,7 @@
     pl.semaphore_wait(barrier, n)
 
     def send_all(source, target, send_sem, recv_sem, h):
-        @pl.loop(1, n)
-        def _(k):
-            d = at_offset(me, k, n)
+        def send_to(d):
             pltpu.make_async_remote_copy(
                 src_ref=source.at[h, d],
                 dst_ref=target.at[h, me],
@@ -94,6 +100,8 @@
                 device_id={"wave": d},
                 device_id_type=MESH,
             ).start()
+
+        each_peer(me, n, send_to)
 
     def all_of(source, target, send_sem, recv_sem, h):
         return pltpu.make_async_remote_copy(
@@ -233,6 +241,16 @@
         own_out(h).wait()
         all_of(send, recv, in_send, in_recv, h).wait_send()
         all_of(send_out, result, out_send, out_recv, h).wait()
+
+
+def row_kernel(n, columns_ref, rows_ref):
+    for h in range(2):
+
+        @pl.loop(0, n // 8, unroll=True)
+        def _(t):
+            for r in range(8):
+                rows = columns_ref[h, pl.ds(t * 64 + r, 8, stride=8), :]
+                rows_ref[pl.ds(r * n + t * 8, 8), pl.ds(h * LANES, LANES)] = rows
 
 
 def per_device(
@@ -296,7 +314,14 @@
         mode_in,
         mode_out,
     )
-    return out.transpose(2, 1, 0, 3).reshape(1, 8, n, 2 * LANES)
+    rows = pl.pallas_call(
+        functools.partial(row_kernel, n),
+        out_shape=jax.ShapeDtypeStruct((8 * n, 2 * LANES), f32),
+        in_specs=[vmem],
+        out_specs=vmem,
+        name="latitude_rows",
+    )(out.reshape(2, 8 * n, LANES))
+    return rows.reshape(1, 8, n, 2 * LANES)
 
 
 def solution(mesh):

time: 80.2 us -> 73.6 us (0.918)
  Pallas kernels: 76.5 us -> 72.8 us
  local copies, waits for them, and re-layouts: 2.87 us -> 0 us
    pallas_call x1, Pallas kernels: 76.5 us -> 70.4 us  [per_device(): pl.pallas_call(functools.partial(step_kernel, n), out_shape=jax.ShapeDtyp...]
    pallas_call x0 -> x1, Pallas kernels: none -> 2.4 us  [per_device(): pl.pallas_call(functools.partial(row_kernel, n), out_shape=jax.ShapeDtype...]
    transpose x1 -> x0, local copies, waits for them, and re-layouts: 1.56 us -> none  [per_device(): return out.transpose(2, 1, 0, 3).reshape(1, 8, n, 2 * LANES)]
    reshape x1 -> x0, local copies, waits for them, and re-layouts: 1.31 us -> none  [per_device(): return out.transpose(2, 1, 0, 3).reshape(1, 8, n, 2 * LANES)]
where the time goes in v3:
time: 73.6 us; the launch traced here: 73.4 us
  Pallas kernels  72.8 us (99%)
    pallas_call x1, Pallas kernels, per_device(): pl.pallas_call(functools.partial(step_kernel, n), out_shape=jax.ShapeDtyp...  70.4 us
    pallas_call x1, Pallas kernels, per_device(): pl.pallas_call(functools.partial(row_kernel, n), out_shape=jax.ShapeDtype...  2.4 us

profile of v3, /device:TPU:1, one launch (start us, length us, event | category | flops | bytes accessed | tf_op | source)
XLA Modules:
  0.0 73.4 jit_solution(255542107782274994)
XLA Ops:
  0.7 70.4 %spectral_step.1 = f32[2,128,8,128]{3,2,1,0:T(8,128)} custom-call(s32[1]{0:T(128)S(6)} %copy.9.wave_ref, f32[1024,256]{1,0:T(8,128)} %bitcast.9, f32[2000,1024]{1,0:T(8,128)} %bitcast.8, s32[8,128]{1,0:T(8,128)} %bitcast.10, f32[8,128]{1,0:T(8,128)} %bitcast.11, f32[1,128]{1,0:T(1,128)} %bitcast.12, f32[128,128]{1,0:T(8,128)} %in_ref.1, f32[128,128]{1,0:T(8,128)} %out_mat_ref.1), custom_call_target="tpu_custom_call" | custom-call | flops 6291456000 | bytes 8192000 | tf_op jit(solution)/shard_map/spectral_step/pallas_call | solution.py:268
  71.0 2.4 %latitude_rows.1 = f32[1024,256]{1,0:T(8,128)} custom-call(f32[2,1024,128]{2,1,0:T(8,128)} %bitcast.7), custom_call_target="tpu_custom_call" | custom-call | tf_op jit(solution)/shard_map/latitude_rows/pallas_call | solution.py:317

commit v4 on v3

--- a/solution.py
+++ b/solution.py
@@ -113,8 +113,7 @@
             device_id_type=MESH,
         )
 
-    for h in range(2):
-        send_all(send, recv, in_send, in_recv, h)
+    send_all(send, recv, in_send, in_recv, 0)
 
     for t in range(lats // LANES):
         rows = pl.ds(t * LANES, LANES)
@@ -226,13 +225,14 @@
     def own_out(h):
         return pltpu.make_async_copy(send_out.at[h, me], result.at[h, me], own_sem.at[h])
 
+    send_all(send, recv, in_send, in_recv, 1)
     all_of(send, recv, in_send, in_recv, 0).wait_recv()
     pair_of(0).start()
     pair_of(0).wait()
     solve(0)
-    send_back(0)
     all_of(send, recv, in_send, in_recv, 1).wait_recv()
     pair_of(1).start()
+    send_back(0)
     pair_of(1).wait()
     solve(1)
     send_back(1)

time: 73.6 us -> 72.3 us (0.982)
  Pallas kernels: 72.8 us -> 71.3 us
    pallas_call x1, Pallas kernels: 70.4 us -> 68.9 us  [per_device(): pl.pallas_call(functools.partial(step_kernel, n), out_shape=jax.ShapeDtyp...]
where the time goes in v4:
time: 72.3 us; the launch traced here: 72 us
  Pallas kernels  71.3 us (99%)
    pallas_call x1, Pallas kernels, per_device(): pl.pallas_call(functools.partial(step_kernel, n), out_shape=jax.ShapeDtyp...  68.9 us
    pallas_call x1, Pallas kernels, per_device(): pl.pallas_call(functools.partial(row_kernel, n), out_shape=jax.ShapeDtype...  2.4 us

profile of v4, /device:TPU:1, one launch (start us, length us, event | category | flops | bytes accessed | tf_op | source)
XLA Modules:
  0.0 72.0 jit_solution(7943532423626605118)
XLA Ops:
  0.7 68.9 %spectral_step.1 = f32[2,128,8,128]{3,2,1,0:T(8,128)} custom-call(s32[1]{0:T(128)S(6)} %copy.9.wave_ref, f32[1024,256]{1,0:T(8,128)} %bitcast.9, f32[2000,1024]{1,0:T(8,128)} %bitcast.8, s32[8,128]{1,0:T(8,128)} %bitcast.10, f32[8,128]{1,0:T(8,128)} %bitcast.11, f32[1,128]{1,0:T(1,128)} %bitcast.12, f32[128,128]{1,0:T(8,128)} %in_ref.1, f32[128,128]{1,0:T(8,128)} %out_mat_ref.1), custom_call_target="tpu_custom_call" | custom-call | flops 6291456000 | bytes 8192000 | tf_op jit(solution)/shard_map/spectral_step/pallas_call | solution.py:268
  69.6 2.4 %latitude_rows.1 = f32[1024,256]{1,0:T(8,128)} custom-call(f32[2,1024,128]{2,1,0:T(8,128)} %bitcast.7), custom_call_target="tpu_custom_call" | custom-call | tf_op jit(solution)/shard_map/latitude_rows/pallas_call | solution.py:317
